TPU v7x, 128 devices: a whole 4x4x4 slice. The times are simulated.
128 devices in a mesh: fsdp: 2 (over y_hi), tile: 32 (over z, x, core), scan: 2 (over y_lo).
Axes of the slice: x: 4, y: 4 (y_hi: 2, y_lo: 2; y = y_hi * 2 + y_lo), z: 4, core: 2. Of those that a mesh axis runs over, the one named last changes fastest.
Arguments:
- acts: bfloat16 [2, 2, 16, 64, 64, 512], P('scan', 'fsdp', None, 'tile'), may hold values from -6 to 6
- spatial_weight: bfloat16 [9, 512, 512], P(None, None, 'fsdp'), may hold values from -0.09375 to 0.09375
- temporal_weight: bfloat16 [3, 512, 512], P(None, None, 'fsdp'), may hold values from -0.15625 to 0.15625
- readout_weight: bfloat16 [2, 4096, 512], P('scan', 'tile'), may hold values from -0.25 to 0.25
- readout_bias: bfloat16 [2, 4096], P('scan', 'tile'), may hold values from -1.5 to 0.5
- tile_of: int32 [2, 4096, 1], P('scan', 'tile'), may hold values from 0 to 31; in each aligned block of 128 rows (0 to 127, 128 to 255, ..., all dimensions but the last counted through in order) at most 10 rows name the same one
- row_of: int32 [2, 4096], P('scan', 'tile'), may hold values from 0 to 1
- column_of: int32 [2, 4096], P('scan', 'tile'), may hold values from 0 to 63
- spikes: int32 [2, 2, 16, 4096], P('scan', 'fsdp', None, 'tile'), may hold values from 0 to 5
Outputs:
- spatial_grad: float32 [9, 512, 512], P(None, None, 'fsdp')
- temporal_grad: float32 [3, 512, 512], P(None, None, 'fsdp')
- readout_grad: float32 [2, 4096, 512], P('scan', 'tile')
- bias_grad: float32 [2, 4096], P('scan', 'tile')
Inputs may be any that keep to these rules, and one draw needn't show every extreme that they name: `tile_of`: among the 128 neurons of one index of tile (aligned blocks of a scan's neurons), at most 10 read one tile.
All inputs are finite; a program needn't handle non-finite values.
Results may differ from a plain program's by a relative error of at most 0.006.
Values may be sent and summed in bfloat16 or wider, within the bound.
No kernel may reach another device: no remote copies, remote signals or barrier semaphores. Data moves between devices by JAX's collectives and lax.ppermute only.
A program may use at most 192 MiB of HBM per device.

v0:
```python
import jax
import jax.numpy as jnp
from jax import lax
from jax.sharding import PartitionSpec as P


def padded_2(block, sides, width):
    for axis, dim in sides:
        count = lax.axis_size(axis)
        forward = [(i, i + 1) for i in range(count - 1)]
        backward = [(target, source) for source, target in forward]
        low = lax.ppermute(
            lax.slice_in_dim(block, block.shape[dim] - width, None, axis=dim), axis, forward
        )
        high = lax.ppermute(lax.slice_in_dim(block, 0, width, axis=dim), axis, backward)
        block = jnp.concatenate([low, block, high], axis=dim)
    return block


def contract_rows(left, right):
    return lax.dot_general(
        left, right, (((0,), (0,)), ((), ())), preferred_element_type=jnp.float32
    )


def on_device(
    acts,
    spatial_weight,
    temporal_weight,
    readout_weight,
    readout_bias,
    tile_of,
    row_of,
    column_of,
    spikes,
):
    spatial, temporal = (
        lax.all_gather(spatial_weight, "fsdp", axis=2, tiled=True),
        lax.all_gather(temporal_weight, "fsdp", axis=2, tiled=True),
    )
    frames_in = acts[0, 0]
    frames, rows, width, channels = frames_in.shape
    cells = rows * width
    extended = padded_2(frames_in, (("tile", 1),), 1)
    padded = jnp.pad(extended, ((0, 0), (0, 0), (1, 1), (0, 0)))

    def patch(tap):
        return padded[:, tap // 3 : tap // 3 + rows, tap % 3 : tap % 3 + width, :].reshape(
            -1, channels
        )

    spatial_sum = jnp.zeros((frames * cells, channels), jnp.float32)
    for tap in range(9):
        spatial_sum = spatial_sum + jnp.dot(
            patch(tap), spatial[tap], preferred_element_type=jnp.float32
        )
    spatial_out = spatial_sum.astype(jnp.bfloat16).reshape(frames, cells, channels)
    causal = jnp.pad(spatial_out, ((2, 0), (0, 0), (0, 0)))
    mixed = jnp.zeros((frames * cells, channels), jnp.float32)
    for lag in range(3):
        mixed = mixed + jnp.dot(
            causal[2 - lag : 2 - lag + frames].reshape(-1, channels),
            temporal[lag],
            preferred_element_type=jnp.float32,
        )
    mixed = mixed.reshape(frames, cells, channels)
    features = jax.nn.elu(mixed).astype(jnp.bfloat16)
    tile_count = lax.axis_size("tile")
    rep_count = lax.axis_size("fsdp")
    neurons = readout_weight.shape[1]
    capacity = max(2, 5 * neurons // (2 * tile_count))
    slot_count = tile_count * capacity
    scale_factor = 1.0 / (rep_count * frames)
    tile_ids = tile_of[0, :, 0]
    cell_ids = row_of[0] * width + column_of[0]
    onehot_tile = (tile_ids[:, None] == jnp.arange(tile_count)[None, :]).astype(jnp.int32)
    earlier = jnp.cumsum(onehot_tile, axis=0) - onehot_tile
    rank_ids = jnp.sum(earlier * onehot_tile, axis=1)
    slot_ids = tile_ids * capacity + rank_ids
    selector = slot_ids[None, :] == jnp.arange(slot_count)[:, None]
    weights_now = readout_weight[0]
    bias_now = readout_bias[0].astype(jnp.float32)
    counts_now = spikes[0, 0]
    wanted = jnp.sum(jnp.where(selector, cell_ids[None, :], 0), axis=1).reshape(
        tile_count, capacity
    )
    held_cells = lax.all_to_all(wanted, "tile", split_axis=0, concat_axis=0, tiled=True).reshape(-1)
    outgoing = features[:, held_cells, :].reshape(frames, tile_count, capacity, channels)
    arrived = lax.all_to_all(outgoing, "tile", split_axis=1, concat_axis=1, tiled=True).reshape(
        frames, slot_count, channels
    )
    picked = arrived[:, slot_ids, :]
    logits = (
        jnp.einsum("fnc,nc->fn", picked, weights_now, preferred_element_type=jnp.float32)
        + bias_now[None, :]
    )
    delta = (jnp.exp(logits) - counts_now.astype(jnp.float32)) * scale_factor
    weight_grad = jnp.einsum("fn,fnc->nc", delta, picked.astype(jnp.float32))
    bias_grad = jnp.sum(delta, axis=0)
    terms = (delta[:, :, None] * weights_now[None, :, :].astype(jnp.float32)).astype(jnp.bfloat16)
    placed = jnp.einsum(
        "sn,fnc->fsc", selector.astype(jnp.bfloat16), terms, preferred_element_type=jnp.float32
    ).astype(jnp.bfloat16)
    returned = lax.all_to_all(
        placed.reshape(frames, tile_count, capacity, channels),
        "tile",
        split_axis=1,
        concat_axis=1,
        tiled=True,
    )
    returned = returned.reshape(frames, slot_count, channels)
    scatter_table = (jnp.arange(cells)[:, None] == held_cells[None, :]).astype(jnp.bfloat16)
    feature_grad = jnp.einsum(
        "ks,fsc->fkc", scatter_table, returned, preferred_element_type=jnp.float32
    )
    weight_grad, bias_grad = lax.psum((weight_grad, bias_grad), "fsdp")
    slope = jnp.where(mixed > 0, 1.0, jnp.exp(jnp.minimum(mixed, 0.0)))
    mixed_grad = (feature_grad * slope).astype(jnp.bfloat16)
    flat_grad = mixed_grad.reshape(-1, channels)
    temporal_grad = jnp.stack(
        [
            contract_rows(causal[2 - lag : 2 - lag + frames].reshape(-1, channels), flat_grad)
            for lag in range(3)
        ]
    )
    back_pad = jnp.pad(mixed_grad, ((0, 2), (0, 0), (0, 0)))
    spatial_back = jnp.zeros((frames * cells, channels), jnp.float32)
    for lag in range(3):
        spatial_back = spatial_back + lax.dot_general(
            back_pad[lag : lag + frames].reshape(-1, channels),
            temporal[lag],
            (((1,), (1,)), ((), ())),
            preferred_element_type=jnp.float32,
        )
    spatial_back = spatial_back.astype(jnp.bfloat16)
    spatial_grad = jnp.stack([contract_rows(patch(tap), spatial_back) for tap in range(9)])
    shard_spatial, shard_temporal = (
        lax.psum_scatter(spatial_grad, "fsdp", scatter_dimension=2, tiled=True),
        lax.psum_scatter(temporal_grad, "fsdp", scatter_dimension=2, tiled=True),
    )
    total_spatial, total_temporal = lax.psum((shard_spatial, shard_temporal), ("tile", "scan"))
    return (total_spatial, total_temporal, weight_grad[None], bias_grad[None])


def solution(mesh):
    return jax.shard_map(
        on_device,
        mesh=mesh,
        in_specs=(
            P("scan", "fsdp", None, "tile", None, None),
            P(None, None, "fsdp"),
            P(None, None, "fsdp"),
            P("scan", "tile", None),
            P("scan", "tile"),
            P("scan", "tile", None),
            P("scan", "tile"),
            P("scan", "tile"),
            P("scan", "fsdp", None, "tile"),
        ),
        out_specs=(
            P(None, None, "fsdp"),
            P(None, None, "fsdp"),
            P("scan", "tile", None),
            P("scan", "tile"),
        ),
        check_vma=False,
    )
```

profile of v0, /device:TPU:1, one launch (start us, length us, event | category | flops | bytes accessed | tf_op | source)
XLA Modules:
  0.0 1104.2 jit_solution(8402206730829438454)
XLA Ops:
  10.3 4.5 collective-permute-start
  18.1 8.6 all-to-all-start
  27.4 7.7 all-to-all-done
  36.5 3.5 fusion.7
  40.0 6.6 fusion.56
  46.7 3.6 pad_maximum_fusion.2
  50.2 29.1 %all-gather.3.cloned.1.call-done = bf16[9,512,512]{2,1,0:T(8,128)(2,1)} async-done(((bf16[9,512,256]{2,1,0:T(8,128)(2,1)}), bf16[9,512,512]{2,1,0:T(8,128)(2,1)}) %all-gather.3.cloned.1.call-update) | async-done | bytes 4718608 | tf_op jit(solution)/shard_map/all_gather | solution.py:38
  84.7 3.3 fusion.34
  88.1 3.2 fusion.35
  91.3 3.3 fusion.37
  94.5 3.3 fusion.30
  97.8 3.3 fusion.36
  101.1 3.3 fusion.33
  104.4 10.9 add_convert_fusion.1
  115.3 4.4 copy.22
  119.7 4.6 pad_slice_fusion.2
  124.2 3.9 copy.23
  128.1 3.9 copy.24
  142.6 5.2 gather_fusion
  147.8 8.4 all-to-all-start.1
  156.3 61.6 %all-to-all-done.1 = bf16[16,32,10,512]{3,0,2,1:T(8,128)(2,1)} async-done(((bf16[16,32,10,512]{3,0,2,1:T(8,128)(2,1)}), bf16[16,32,10,512]{3,0,2,1:T(8,128)(2,1)}, u32[]{:S(2)}, u32[]{:S(2)}) %all-to-all-start.1) | async-done | bytes 5242912 | tf_op jit(solution)/shard_map/all_to_all | solution.py:89
  217.9 4.5 gather_fusion.1
  226.5 5.3 copy.27
  231.8 8.7 all-to-all-start.2
  240.6 61.8 %all-to-all-done.2 = bf16[16,32,10,512]{3,0,2,1:T(8,128)(2,1)} async-done(((bf16[16,32,10,512]{3,0,2,1:T(8,128)(2,1)}), bf16[16,32,10,512]{3,0,2,1:T(8,128)(2,1)}, u32[]{:S(2)}, u32[]{:S(2)}) %all-to-all-start.2) | async-done | bytes 5242912 | tf_op jit(solution)/shard_map/all_to_all | solution.py:104
  302.4 8.1 fusion.11
  347.5 14.7 %reduce-scatter.5.cloned.1.call-done = f32[3,512,256]{2,1,0:T(8,128)} async-done(((f32[3,512,512]{2,1,0:T(8,128)}), f32[3,512,256]{2,1,0:T(8,128)}) %reduce-scatter.5.cloned.1.call-update) | async-done | bytes 1572880 | tf_op jit(solution)/shard_map/reduce_scatter | solution.py:139
  362.2 116.4 %reduce-scatter.3.cloned.1.call-done = f32[9,512,256]{2,1,0:T(8,128)} async-done(((f32[9,512,512]{2,1,0:T(8,128)}), f32[9,512,256]{2,1,0:T(8,128)}) %reduce-scatter.3.cloned.1.call-update) | async-done | bytes 4718608 | tf_op jit(solution)/shard_map/reduce_scatter | solution.py:138
  478.6 5.8 psum.31
  484.4 27.5 %all-reduce.7.cloned.1.call-done = f32[1,128,512]{2,1,0:T(8,128)} async-done(((f32[1,128,512]{2,1,0:T(8,128)}), f32[1,128,512]{2,1,0:T(8,128)}) %all-reduce.7.cloned.1.call-update) | async-done | bytes 262160 | tf_op jit(solution)/shard_map/psum | solution.py:116
  511.9 578.2 %all-reduce.9.cloned.1.call-done = (f32[9,512,256]{2,1,0:T(8,128)}, f32[3,512,256]{2,1,0:T(8,128)}) async-done(((f32[9,512,256]{2,1,0:T(8,128)}, f32[3,512,256]{2,1,0:T(8,128)}), (f32[9,512,256]{2,1,0:T(8,128)}, f32[3,512,256]{2,1,0:T(8,128)})) %all-reduce.9.cloned.1.call-update) | async-done | bytes 6291472 | tf_op jit(solution)/shard_map/psum | solution.py:141
  1090.1 4.9 copy.54
  (135 shorter events, 67.2 us)
Async XLA Ops:
  7.2 72.2 %all-gather.3.cloned.1.call-start = ((), (), s32[]{:S(2)}) async-start(), calls=%async_computation.5 | async-start | bytes 7077888 | tf_op jit(solution)/shard_map/all_gather | solution.py:38
  8.8 8.0 copy-start.30
  8.8 8.4 copy-start.31
  8.8 8.4 copy-start.32
  10.3 26.2 %collective-permute-start = (bf16[16,1,64,512]{3,2,1,0:T(8,128)(2,1)}, bf16[16,1,64,512]{3,2,1,0:T(8,128)(2,1)S(1)}, u32[]{:S(2)}, u32[]{:S(2)}) collective-permute-start(bf16[16,1,64,512]{3,2,1,0:T(8,128)(2,1)} %get-tuple-element.20), channel_id=1, source_target_pairs={{0,2},{2,4},{4,6},{6,8},{8,10},{10,12},{12,14},{14,16},{16,18},{18... | collective-permute-start | bytes 3145736 | tf_op jit(solution)/shard_map/ppermute | solution.py:12
  14.8 21.7 %collective-permute-start.1 = (bf16[16,1,64,512]{3,2,1,0:T(8,128)(2,1)}, bf16[16,1,64,512]{3,2,1,0:T(8,128)(2,1)}, u32[]{:S(2)}, u32[]{:S(2)}) collective-permute-start(bf16[16,1,64,512]{3,2,1,0:T(8,128)(2,1)} %get-tuple-element.21), channel_id=1, source_target_pairs={{2,0},{4,2},{6,4},{8,6},{10,8},{12,10},{14,12},{16,14},{18,16},{20... | collective-permute-start | bytes 3145736 | tf_op jit(solution)/shard_map/ppermute | solution.py:15
  18.1 17.0 %all-to-all-start = ((s32[32,1,10]{2,1,0:T(1,128)}), s32[32,1,10]{2,1,0:T(1,128)S(1)}, u32[]{:S(2)}, u32[]{:S(2)}) async-start(s32[32,1,10]{2,1,0:T(1,128)} %bitcast.28), calls=%async_computation | async-start | bytes 32768 | tf_op jit(solution)/shard_map/all_to_all | solution.py:87
  26.7 105.4 %all-gather.5.cloned.1.call-start = ((), (), s32[]{:S(2)}) async-start(), calls=%async_computation.6 | async-start | bytes 2359296 | tf_op jit(solution)/shard_map/all_gather | solution.py:39
  79.3 3.1 copy-start.6
  79.3 3.8 copy-start.25
  84.7 3.3 copy-start.10
  88.0 3.2 copy-start.12
  91.3 3.3 copy-start.15
  94.5 3.3 copy-start.17
  101.1 3.3 copy-start.19
  132.1 3.1 copy-start.14
  132.1 3.1 copy-start.23
  147.8 8.4 copy-start.33
  147.8 8.4 copy-start.28
  147.8 70.1 %all-to-all-start.1 = ((bf16[16,32,10,512]{3,0,2,1:T(8,128)(2,1)}), bf16[16,32,10,512]{3,0,2,1:T(8,128)(2,1)}, u32[]{:S(2)}, u32[]{:S(2)}) async-start(bf16[16,32,10,512]{3,0,2,1:T(8,128)(2,1)} %bitcast.218), calls=%async_computation.1 | async-start | bytes 10485760 | tf_op jit(solution)/shard_map/all_to_all | solution.py:89
  222.4 2.4 copy-start.29
  231.8 70.6 %all-to-all-start.2 = ((bf16[16,32,10,512]{3,0,2,1:T(8,128)(2,1)}), bf16[16,32,10,512]{3,0,2,1:T(8,128)(2,1)}, u32[]{:S(2)}, u32[]{:S(2)}) async-start(bf16[16,32,10,512]{3,0,2,1:T(8,128)(2,1)} %bitcast.219), calls=%async_computation.2 | async-start | bytes 10485760 | tf_op jit(solution)/shard_map/all_to_all | solution.py:104
  240.5 121.7 %reduce-scatter.5.cloned.1.call-start = ((), (), s32[]{:S(2)}) async-start(), calls=%async_computation.8 | async-start | bytes 4718592 | tf_op jit(solution)/shard_map/reduce_scatter | solution.py:139
  302.4 8.1 copy-start.1
  310.5 2.5 copy-start.3
  316.4 162.3 %reduce-scatter.3.cloned.1.call-start = ((), (), s32[]{:S(2)}) async-start(), calls=%async_computation.7 | async-start | bytes 14155776 | tf_op jit(solution)/shard_map/reduce_scatter | solution.py:138
  316.6 2.7 copy-start.4
  316.6 3.2 copy-start.24
  340.0 2.3 copy-start.20
  344.6 167.3 %all-reduce.7.cloned.1.call-start = ((), (), s32[]{:S(2)}) async-start(), calls=%async_computation.9 | async-start | bytes 524288 | tf_op jit(solution)/shard_map/psum | solution.py:116
  347.5 742.7 %all-reduce.9.cloned.1.call-start = ((), (), s32[]{:S(2)}) async-start(), calls=%async_computation.10 | async-start | bytes 12582912 | tf_op jit(solution)/shard_map/psum | solution.py:141
  1090.1 4.9 copy-start.26
  (13 other events, 25.0 us)
Sparse Core Ops, SparseCore 0:
  9.6 69.6 all-gather.2
  81.0 30.5 all-gather.4
  316.5 45.6 reduce-scatter.4
  364.5 114.0 reduce-scatter.2
  481.5 30.4 all-reduce.6
  514.3 575.7 all-reduce.8
where the time goes:
time: 1110 us; the launch traced here: 1100 us
  waiting for transfers between devices  899 us (81%)
  matrix products  81.2 us (7%)
  local copies, waits for them, and re-layouts  59.2 us (5%)
  starting transfers between devices  32.5 us (3%)
  between operations  14.9 us (1%)
  other arithmetic  12 us (1%)
    psum x1, waiting for transfers between devices, on_device(): lax.psum((shard_spatial, shard_temporal), ('tile', 'scan'))  578 us
    reduce_scatter x1, waiting for transfers between devices, on_device(): lax.psum_scatter(spatial_grad, 'fsdp', scatter_dimension=2, tiled=True)  116 us
    all_to_all x1, waiting for transfers between devices, on_device(): lax.all_to_all(placed.reshape(frames, tile_count, capacity, channels), 't...  61.8 us
    all_to_all x1, waiting for transfers between devices, on_device(): lax.all_to_all(outgoing, 'tile', split_axis=1, concat_axis=1, tiled=True)  61.6 us
    dot_general x9, matrix products, on_device(): jnp.dot(patch(tap), spatial[tap], preferred_element_type=jnp.float32)  34.9 us
    all_gather x1, waiting for transfers between devices, on_device(): lax.all_gather(spatial_weight, 'fsdp', axis=2, tiled=True)  29.1 us
    psum x1, waiting for transfers between devices, on_device(): weight_grad, bias_grad = lax.psum((weight_grad, bias_grad), 'fsdp')  27.5 us
    dot_general x12, matrix products, contract_rows(): lax.dot_general(left, right, (((0,), (0,)), ((), ())), preferred_element_...  24.2 us
  transfers between devices with their start and end apart: 11, of which 8 were waited for; matrix products, arithmetic and copies ran while one was open for 9% of the time, Pallas kernels for 0%

commit v1 on v0

--- a/solution.py
+++ b/solution.py
@@ -2,6 +2,7 @@
 import jax.numpy as jnp
 from jax import lax
 from jax.sharding import PartitionSpec as P
+from jax.lax import all_to_all, axis_size
 
 
 def padded_2(block, sides, width):
@@ -101,13 +102,16 @@
     placed = jnp.einsum(
         "sn,fnc->fsc", selector.astype(jnp.bfloat16), terms, preferred_element_type=jnp.float32
     ).astype(jnp.bfloat16)
-    returned = lax.all_to_all(
-        placed.reshape(frames, tile_count, capacity, channels),
-        "tile",
-        split_axis=1,
-        concat_axis=1,
-        tiled=True,
-    )
+
+    def _make_hubs(piece_in, axis_no, join_dim):
+        return jnp.concatenate(
+            all_to_all(
+                jnp.stack(jnp.split(piece_in, axis_size("tile"), axis_no), axis=0), "tile", 0, 0
+            ),
+            join_dim,
+        )
+
+    returned = _make_hubs(placed.reshape(frames, tile_count, capacity, channels), 1, 1)
     returned = returned.reshape(frames, slot_count, channels)
     scatter_table = (jnp.arange(cells)[:, None] == held_cells[None, :]).astype(jnp.bfloat16)
     feature_grad = jnp.einsum(

time: 1110 us -> 1140 us (1.027)
  local copies, waits for them, and re-layouts: 59.2 us -> 80.8 us
    unnamed x71 -> x102, local copies, waits for them, and re-layouts: 11.8 us -> 33.5 us
where the time goes in v1:
time: 1140 us; the launch traced here: 1130 us
  waiting for transfers between devices  898 us (79%)
  matrix products  81.2 us (7%)
  local copies, waits for them, and re-layouts  80.8 us (7%)
  starting transfers between devices  32.7 us (3%)
  between operations  15 us (1%)
  other arithmetic  12 us (1%)
    psum x1, waiting for transfers between devices, on_device(): lax.psum((shard_spatial, shard_temporal), ('tile', 'scan'))  578 us
    reduce_scatter x1, waiting for transfers between devices, on_device(): lax.psum_scatter(spatial_grad, 'fsdp', scatter_dimension=2, tiled=True)  116 us
    all_to_all x1, waiting for transfers between devices, on_device(): lax.all_to_all(outgoing, 'tile', split_axis=1, concat_axis=1, tiled=True)  61.6 us
    all_to_all x1, waiting for transfers between devices, _make_hubs(): all_to_all(jnp.stack(jnp.split(piece_in, axis_size('tile'), axis_no), axi...  61.5 us
    dot_general x9, matrix products, on_device(): jnp.dot(patch(tap), spatial[tap], preferred_element_type=jnp.float32)  34.9 us
    unnamed x102, local copies, waits for them, and re-layouts  33.5 us
    all_gather x1, waiting for transfers between devices, on_device(): lax.all_gather(spatial_weight, 'fsdp', axis=2, tiled=True)  28.4 us
    psum x1, waiting for transfers between devices, on_device(): weight_grad, bias_grad = lax.psum((weight_grad, bias_grad), 'fsdp')  27.5 us
  transfers between devices with their start and end apart: 11, of which 8 were waited for; matrix products, arithmetic and copies ran while one was open for 9% of the time, Pallas kernels for 0%

profile of v1, /device:TPU:1, one launch (start us, length us, event | category | flops | bytes accessed | tf_op | source)
XLA Modules:
  0.0 1125.1 jit_solution(4054040922854783619)
XLA Ops:
  7.9 3.1 fusion.89
  11.0 4.5 collective-permute-start
  18.8 8.6 all-to-all-start
  28.1 7.7 all-to-all-done
  37.2 3.5 fusion.7
  40.8 6.6 fusion.88
  47.4 3.6 pad_maximum_fusion.2
  50.9 28.4 %all-gather.3.cloned.1.call-done = bf16[9,512,512]{2,1,0:T(8,128)(2,1)} async-done(((bf16[9,512,256]{2,1,0:T(8,128)(2,1)}), bf16[9,512,512]{2,1,0:T(8,128)(2,1)}) %all-gather.3.cloned.1.call-update) | async-done | bytes 4718608 | tf_op jit(solution)/shard_map/all_gather | solution.py:39
  84.7 3.3 fusion.34
  88.1 3.2 fusion.35
  91.3 3.3 fusion.37
  94.6 3.3 fusion.30
  97.9 3.3 fusion.36
  101.2 3.3 fusion.33
  104.4 10.9 add_convert_fusion.1
  115.4 4.4 copy.54
  119.7 4.6 pad_slice_fusion.2
  124.3 3.9 copy.55
  128.2 3.9 copy.56
  144.2 5.2 gather_fusion
  149.4 8.4 all-to-all-start.1
  157.9 61.6 %all-to-all-done.1 = bf16[16,32,10,512]{3,0,2,1:T(8,128)(2,1)} async-done(((bf16[16,32,10,512]{3,0,2,1:T(8,128)(2,1)}), bf16[16,32,10,512]{3,0,2,1:T(8,128)(2,1)}, u32[]{:S(2)}, u32[]{:S(2)}) %all-to-all-start.1) | async-done | bytes 5242912 | tf_op jit(solution)/shard_map/all_to_all | solution.py:90
  219.5 4.5 gather_fusion.1
  252.7 8.7 all-to-all-start.2
  261.7 61.5 %all-to-all-done.2 = bf16[32,16,1,10,512]{4,1,3,2,0:T(8,128)(2,1)} async-done(((bf16[32,16,1,10,512]{4,1,3,2,0:T(8,128)(2,1)}), bf16[32,16,1,10,512]{4,1,3,2,0:T(8,128)(2,1)}, u32[]{:S(2)}, u32[]{:S(2)}) %all-to-all-start.2) | async-done | bytes 5242912 | tf_op jit(solution)/shard_map/all_to_all | solution.py:108
  323.3 8.1 fusion.11
  368.4 14.7 %reduce-scatter.5.cloned.1.call-done = f32[3,512,256]{2,1,0:T(8,128)} async-done(((f32[3,512,512]{2,1,0:T(8,128)}), f32[3,512,256]{2,1,0:T(8,128)}) %reduce-scatter.5.cloned.1.call-update) | async-done | bytes 1572880 | tf_op jit(solution)/shard_map/reduce_scatter | solution.py:143
  383.1 116.4 %reduce-scatter.3.cloned.1.call-done = f32[9,512,256]{2,1,0:T(8,128)} async-done(((f32[9,512,512]{2,1,0:T(8,128)}), f32[9,512,256]{2,1,0:T(8,128)}) %reduce-scatter.3.cloned.1.call-update) | async-done | bytes 4718608 | tf_op jit(solution)/shard_map/reduce_scatter | solution.py:142
  499.5 5.8 psum.31
  505.3 27.5 %all-reduce.7.cloned.1.call-done = f32[1,128,512]{2,1,0:T(8,128)} async-done(((f32[1,128,512]{2,1,0:T(8,128)}), f32[1,128,512]{2,1,0:T(8,128)}) %all-reduce.7.cloned.1.call-update) | async-done | bytes 262160 | tf_op jit(solution)/shard_map/psum | solution.py:120
  532.8 578.2 %all-reduce.9.cloned.1.call-done = (f32[9,512,256]{2,1,0:T(8,128)}, f32[3,512,256]{2,1,0:T(8,128)}) async-done(((f32[9,512,256]{2,1,0:T(8,128)}, f32[3,512,256]{2,1,0:T(8,128)}), (f32[9,512,256]{2,1,0:T(8,128)}, f32[3,512,256]{2,1,0:T(8,128)})) %all-reduce.9.cloned.1.call-update) | async-done | bytes 6291472 | tf_op jit(solution)/shard_map/psum | solution.py:145
  1111.0 5.0 copy.117
  (167 shorter events, 91.2 us)
Async XLA Ops:
  7.2 30.1 %copy-start = (bf16[1,1,16,2,64,512]{5,4,3,2,1,0:T(8,128)(2,1)S(1)}, bf16[1,1,16,2,64,512]{5,4,3,2,1,0:T(8,128)(2,1)}, u32[]{:S(2)}) copy-start(bf16[1,1,16,2,64,512]{5,4,3,2,1,0:T(8,128)(2,1)} %param.9) | copy-start | bytes 6291460
  7.2 10.3 copy-start.30
  7.2 10.7 copy-start.32
  7.2 10.7 copy-start.31
  7.2 72.2 %all-gather.3.cloned.1.call-start = ((), (), s32[]{:S(2)}) async-start(), calls=%async_computation.5 | async-start | bytes 7077888 | tf_op jit(solution)/shard_map/all_gather | solution.py:39
  11.0 26.2 %collective-permute-start = (bf16[16,1,64,512]{3,2,1,0:T(8,128)(2,1)}, bf16[16,1,64,512]{3,2,1,0:T(8,128)(2,1)S(1)}, u32[]{:S(2)}, u32[]{:S(2)}) collective-permute-start(bf16[16,1,64,512]{3,2,1,0:T(8,128)(2,1)} %get-tuple-element.20), channel_id=1, source_target_pairs={{0,2},{2,4},{4,6},{6,8},{8,10},{10,12},{12,14},{14,16},{16,18},{18... | collective-permute-start | bytes 3145736 | tf_op jit(solution)/shard_map/ppermute | solution.py:13
  15.5 21.7 %collective-permute-start.1 = (bf16[16,1,64,512]{3,2,1,0:T(8,128)(2,1)}, bf16[16,1,64,512]{3,2,1,0:T(8,128)(2,1)}, u32[]{:S(2)}, u32[]{:S(2)}) collective-permute-start(bf16[16,1,64,512]{3,2,1,0:T(8,128)(2,1)} %get-tuple-element.21), channel_id=1, source_target_pairs={{2,0},{4,2},{6,4},{8,6},{10,8},{12,10},{14,12},{16,14},{18,16},{20... | collective-permute-start | bytes 3145736 | tf_op jit(solution)/shard_map/ppermute | solution.py:16
  18.8 17.0 %all-to-all-start = ((s32[32,1,10]{2,1,0:T(1,128)}), s32[32,1,10]{2,1,0:T(1,128)S(1)}, u32[]{:S(2)}, u32[]{:S(2)}) async-start(s32[32,1,10]{2,1,0:T(1,128)} %bitcast.28), calls=%async_computation | async-start | bytes 32768 | tf_op jit(solution)/shard_map/all_to_all | solution.py:88
  27.4 104.7 %all-gather.5.cloned.1.call-start = ((), (), s32[]{:S(2)}) async-start(), calls=%async_computation.6 | async-start | bytes 2359296 | tf_op jit(solution)/shard_map/all_gather | solution.py:40
  79.4 3.1 copy-start.6
  79.4 3.8 copy-start.25
  84.7 3.4 copy-start.10
  88.1 3.2 copy-start.12
  91.3 3.3 copy-start.15
  94.6 3.3 copy-start.17
  101.2 3.3 copy-start.19
  132.1 3.1 copy-start.14
  132.1 3.1 copy-start.23
  149.4 8.4 copy-start.33
  149.4 8.4 copy-start.28
  149.4 70.1 %all-to-all-start.1 = ((bf16[16,32,10,512]{3,0,2,1:T(8,128)(2,1)}), bf16[16,32,10,512]{3,0,2,1:T(8,128)(2,1)}, u32[]{:S(2)}, u32[]{:S(2)}) async-start(bf16[16,32,10,512]{3,0,2,1:T(8,128)(2,1)} %bitcast.380), calls=%async_computation.1 | async-start | bytes 10485760 | tf_op jit(solution)/shard_map/all_to_all | solution.py:90
  157.8 68.6 %copy-start.29 = (s32[1,1,16,128]{3,2,1,0:T(8,128)S(1)}, s32[1,1,16,128]{3,2,1,0:T(8,128)}, u32[]{:S(2)}) copy-start(s32[1,1,16,128]{3,2,1,0:T(8,128)} %param.17) | copy-start | bytes 24580
  252.7 70.6 %all-to-all-start.2 = ((bf16[32,16,1,10,512]{4,1,3,2,0:T(8,128)(2,1)}), bf16[32,16,1,10,512]{4,1,3,2,0:T(8,128)(2,1)}, u32[]{:S(2)}, u32[]{:S(2)}) async-start(bf16[32,16,1,10,512]{4,1,3,2,0:T(8,128)(2,1)} %fusion.43), calls=%async_computation.2 | async-start | bytes 10485760 | tf_op jit(solution)/shard_map/all_to_all | solution.py:108
  261.3 121.7 %reduce-scatter.5.cloned.1.call-start = ((), (), s32[]{:S(2)}) async-start(), calls=%async_computation.8 | async-start | bytes 4718592 | tf_op jit(solution)/shard_map/reduce_scatter | solution.py:143
  323.3 8.1 copy-start.1
  337.2 162.3 %reduce-scatter.3.cloned.1.call-start = ((), (), s32[]{:S(2)}) async-start(), calls=%async_computation.7 | async-start | bytes 14155776 | tf_op jit(solution)/shard_map/reduce_scatter | solution.py:142
  337.5 2.7 copy-start.4
  337.5 3.2 copy-start.24
  365.6 167.2 %all-reduce.7.cloned.1.call-start = ((), (), s32[]{:S(2)}) async-start(), calls=%async_computation.9 | async-start | bytes 524288 | tf_op jit(solution)/shard_map/psum | solution.py:120
  368.4 742.6 %all-reduce.9.cloned.1.call-start = ((), (), s32[]{:S(2)}) async-start(), calls=%async_computation.10 | async-start | bytes 12582912 | tf_op jit(solution)/shard_map/psum | solution.py:145
  1111.0 5.0 copy-start.26
  1111.0 6.1 copy-start.27
  (13 other events, 27.1 us)
Sparse Core Ops, SparseCore 0:
  9.7 69.6 all-gather.2
  81.0 30.5 all-gather.4
  337.3 45.7 reduce-scatter.4
  385.4 114.0 reduce-scatter.2
  502.3 30.4 all-reduce.6
  535.2 575.7 all-reduce.8
